TPU v7x, 256 devices: a whole 4x4x8 slice. The times are simulated.
256 devices in a mesh: blk: 128 (over y, z, x_lo, core), rhs: 2 (over x_hi).
Axes of the slice: x: 4 (x_hi: 2, x_lo: 2; x = x_hi * 2 + x_lo), y: 4, z: 8, core: 2. Of those that a mesh axis runs over, the one named last changes fastest.
Arguments:
- positions: float32 [3, 32768], P(None, 'blk'), may hold values from -1 to 1
- normal_angles: float32 [2, 32768], P(None, 'blk'), may hold values from -3.140625 to 3.140625
- areas: float32 [32768], P('blk'), may hold values from 1 to 6
- densities: float32 [2, 2, 32768], P('rhs', None, 'blk'), may hold values from -6 to 6
- need_owner: int32 [32768, 1], P('blk'), may hold values from 0 to 127; in each aligned block of 256 rows (0 to 255, 256 to 511, ...) at most 8 rows name the same one
- need_slot: int32 [32768], P('blk'), may hold values from 0 to 255
- near_index: int32 [32, 32768], P(None, 'blk'), may hold values from 0 to 255
- near_coef: float32 [2, 32, 32768], P(None, None, 'blk'), may hold values from -2 to 2
Outputs:
- result_field: float32 [2, 2, 32768], P('rhs', None, 'blk')
Inputs may be any that keep to these rules, and one draw needn't show every extreme that they name: `need_owner`: among the 256 entries of one block of targets, at most 8 name the same owner.
All inputs are finite; a program needn't handle non-finite values.
Results may differ from a plain program's by a relative error of at most 0.0003.
Values sent between devices are 32-bit elements; how exact they have to be, the bound alone decides.
A program may use at most 128 MiB of HBM per device.

v0:
```python
import math
import jax
import jax.numpy as jnp
from jax import lax
from jax.sharding import PartitionSpec as P

WAVE = 8.0
COUPLE = 1.0
SOFT = 0.1
TILE = 512


def unit_normals(angles):
    azimuth = angles[0]
    elevation = angles[1]
    return jnp.stack(
        [
            jnp.cos(azimuth) * jnp.cos(elevation),
            jnp.sin(azimuth) * jnp.cos(elevation),
            jnp.sin(elevation),
        ],
        0,
    )


def kernel_tile(targets, geometry):
    offset_vec = targets[:, :, None] - geometry[0:3, None, :]
    distance = jnp.sqrt(jnp.sum(offset_vec * offset_vec, 0) + SOFT * SOFT)
    facing = jnp.sum(offset_vec * geometry[3:6, None, :], 0)
    single = 1.0 / (4.0 * math.pi * distance)
    double = facing * single / (distance * distance)
    phases = WAVE * distance
    cosine = jnp.cos(phases)
    sines = jnp.sin(phases)
    weight = geometry[6][None, :]
    real_part = weight * (double * (cosine + phases * sines) + COUPLE * single * sines)
    imag_part = weight * (double * (sines - phases * cosine) - COUPLE * single * cosine)
    return (real_part, imag_part)


def apply_tile(targets, geometry, sources):
    real_part, imag_part = kernel_tile(targets, geometry)
    highest = lax.Precision.HIGHEST
    src_real = sources[:, 0, :]
    src_imag = sources[:, 1, :]
    out_real = jnp.einsum("ts,rs->rt", real_part, src_real, precision=highest) - jnp.einsum(
        "ts,rs->rt", imag_part, src_imag, precision=highest
    )
    out_imag = jnp.einsum("ts,rs->rt", real_part, src_imag, precision=highest) + jnp.einsum(
        "ts,rs->rt", imag_part, src_real, precision=highest
    )
    return (out_real, out_imag)


def far_block(running, targets, geometry, sources):
    more_real, more_imag = apply_tile(targets, geometry, sources)
    return (running[0] + more_real, running[1] + more_imag)


def far_piece(running, targets, geometry, flat_sources):
    count_rows = geometry.shape[1]
    side_count = flat_sources.shape[0] // 2
    sources = flat_sources.reshape(side_count, 2, count_rows)
    tile_width = math.gcd(count_rows, TILE)
    blocks = count_rows // tile_width
    geo_tiles = geometry.reshape(7, blocks, tile_width).transpose(1, 0, 2)
    src_tiles = sources.reshape(side_count, 2, blocks, tile_width).transpose(2, 0, 1, 3)

    def advance(partial_sums, tile_pair):
        return (far_block(partial_sums, targets, tile_pair[0], tile_pair[1]), None)

    running, _ = lax.scan(advance, running, (geo_tiles, src_tiles))
    return running


def near_field(needed, near_rows, near_terms):
    looked = needed[:, :, near_rows]
    coef_real = near_terms[0]
    coef_imag = near_terms[1]
    near_real = jnp.sum(coef_real * looked[:, 0] - coef_imag * looked[:, 1], 1)
    near_imag = jnp.sum(coef_real * looked[:, 1] + coef_imag * looked[:, 0], 1)
    return (near_real, near_imag)


def on_device(
    positions, normal_angles, areas, densities, need_owner, need_slot, near_index, near_coef
):
    own_rows = positions.shape[1]
    blk_count = lax.axis_size("blk")
    panels_all = own_rows * blk_count
    normals = unit_normals(normal_angles)
    weights = areas * (1.0 / math.sqrt(panels_all))
    geometry = jnp.concatenate([positions, normals, weights[None, :]], 0)
    owners = need_owner[:, 0]
    need_count = need_slot.shape[0]
    send_density = densities.reshape(2 * densities.shape[0], own_rows)
    side_count = send_density.shape[0] // 2
    target_count = positions.shape[1]
    empty_sum = jnp.zeros((side_count, target_count), jnp.float32)
    far_real, far_imag = far_piece(
        (empty_sum, empty_sum),
        positions,
        lax.all_gather(geometry, "blk", axis=1, tiled=True),
        lax.all_gather(send_density, "blk", axis=1, tiled=True),
    )
    near_sides = densities.shape[0]
    capacity = 4 * need_count // blk_count
    owner_ids = jnp.arange(blk_count, dtype=jnp.int32)
    onehot = (owners[:, None] == owner_ids[None, :]).astype(jnp.int32)
    before = jnp.cumsum(onehot, 0) - onehot
    ranks_in = jnp.sum(before * onehot, 1)
    placed = owners * capacity + ranks_in
    requests = (
        jnp.zeros((blk_count * capacity,), jnp.int32)
        .at[placed]
        .set(need_slot)
        .reshape(blk_count, capacity)
    )
    values = densities[
        :, :, lax.all_to_all(requests, "blk", split_axis=0, concat_axis=0, tiled=True)
    ]
    answers = lax.all_to_all(values, "blk", split_axis=2, concat_axis=2, tiled=True)
    needed = answers.reshape(near_sides, 2, blk_count * capacity)[:, :, placed]
    near_real, near_imag = near_field(needed, near_index, near_coef)
    far_real = far_real + near_real
    far_imag = far_imag + near_imag
    field_real = 0.5 * densities[:, 0] + far_real
    field_imag = 0.5 * densities[:, 1] + far_imag
    result_field = jnp.stack([field_real, field_imag], 1)
    return result_field


def solution(mesh):
    in_specs = (
        P(None, "blk"),
        P(None, "blk"),
        P("blk"),
        P("rhs", None, "blk"),
        P("blk", None),
        P("blk"),
        P(None, "blk"),
        P(None, None, "blk"),
    )
    out_specs = P("rhs", None, "blk")
    return jax.shard_map(
        on_device, mesh=mesh, in_specs=in_specs, out_specs=out_specs, check_vma=False
    )
```

profile of v0, /device:TPU:1, one launch (start us, length us, event | category | flops | bytes accessed | tf_op | source)
XLA Modules:
  0.0 703.4 jit_solution(5454243177161245767)
XLA Ops:
  4.9 14.9 %all-to-all-start = ((s32[128,1,8]{2,1,0:T(1,128)}), s32[128,1,8]{2,1,0:T(1,128)S(1)}, u32[]{:S(2)}, u32[]{:S(2)}) async-start(s32[128,1,8]{2,1,0:T(1,128)} %bitcast.14), calls=%async_computation | async-start | bytes 131072 | tf_op jit(solution)/shard_map/all_to_all | solution.py:120
  22.8 160.4 %all_gather.7 = f32[7,32768]{1,0:T(8,128)S(1)} all-gather(f32[7,256]{1,0:T(8,128)S(1)} %concatenate.3), channel_id=1, replica_groups=mesh['blk'=128,'rhs'=2] {'blk'}, dimensions={1}, use_global_device_ids=true | all-gather | bytes 924672 | tf_op jit(solution)/shard_map/all_gather | solution.py:103
  183.2 151.7 %all-gather = f32[1,2,32768]{2,1,0:T(2,128)S(1)} all-gather(f32[1,2,256]{2,1,0:T(2,128)S(1)} %copy-done.2), channel_id=2, replica_groups=mesh['blk'=128,'rhs'=2] {'blk'}, dimensions={2}, use_global_device_ids=true | all-gather | bytes 264192 | tf_op jit(solution)/shard_map/all_gather | solution.py:104
  334.9 313.9 %while.13 = (s32[]{:T(128)}, f32[1,256]{1,0:T(1,128)S(1)}, f32[1,256]{1,0:T(1,128)S(1)}, f32[64,1,2,512]{3,2,1,0:T(2,128)S(1)}, f32[64,7,512]{2,1,0:T(8,128)S(1)...) while((s32[]{:T(128)}, f32[1,256]{1,0:T(1,128)S(1)}, f32[1,256]{1,0:T(1,128)S(1)}, ...), condition=%wide.region_3.4_spmd.clone, body=%wide.region_0.3_spmd.clone.sunk | while | flops 10487301 | bytes 5321883 | solution.py:72
  335.3 2.4 subtract_multiply_fusion.4
  340.2 2.4 subtract_multiply_fusion.4
  345.1 2.4 subtract_multiply_fusion.4
  350.0 2.4 subtract_multiply_fusion.4
  354.9 2.4 subtract_multiply_fusion.4
  359.8 2.4 subtract_multiply_fusion.4
  364.7 2.4 subtract_multiply_fusion.4
  369.6 2.4 subtract_multiply_fusion.4
  374.5 2.4 subtract_multiply_fusion.4
  384.4 2.4 subtract_multiply_fusion.4
  389.3 2.4 subtract_multiply_fusion.4
  394.2 2.4 subtract_multiply_fusion.4
  399.1 2.4 subtract_multiply_fusion.4
  404.0 2.4 subtract_multiply_fusion.4
  408.9 2.4 subtract_multiply_fusion.4
  413.8 2.4 subtract_multiply_fusion.4
  418.7 2.4 subtract_multiply_fusion.4
  423.6 2.4 subtract_multiply_fusion.4
  428.5 2.4 subtract_multiply_fusion.4
  433.4 2.4 subtract_multiply_fusion.4
  438.3 2.4 subtract_multiply_fusion.4
  443.2 2.4 subtract_multiply_fusion.4
  448.1 2.4 subtract_multiply_fusion.4
  453.0 2.4 subtract_multiply_fusion.4
  457.9 2.4 subtract_multiply_fusion.4
  462.8 2.4 subtract_multiply_fusion.4
  467.7 2.4 subtract_multiply_fusion.4
  477.6 2.4 subtract_multiply_fusion.4
  482.5 2.4 subtract_multiply_fusion.4
  487.4 2.4 subtract_multiply_fusion.4
  492.3 2.4 subtract_multiply_fusion.4
  497.2 2.4 subtract_multiply_fusion.4
  502.1 2.4 subtract_multiply_fusion.4
  507.0 2.4 subtract_multiply_fusion.4
  511.9 2.4 subtract_multiply_fusion.4
  516.8 2.4 subtract_multiply_fusion.4
  521.7 2.4 subtract_multiply_fusion.4
  526.6 2.4 subtract_multiply_fusion.4
  531.5 2.4 subtract_multiply_fusion.4
  649.2 2.8 gather_fusion
  653.4 5.3 all-to-all-start.1
  658.8 11.9 %all-to-all-done.1 = f32[1,2,128,8]{3,1,0,2:T(2,128)S(1)} async-done(((f32[1,2,128,8]{3,1,0,2:T(2,128)}), f32[1,2,128,8]{3,1,0,2:T(2,128)S(1)}, u32[]{:S(2)}, u32[]{:S(2)}) %all-to-all-start.1) | async-done | bytes 8224 | tf_op jit(solution)/shard_map/all_to_all | solution.py:122
  672.2 27.7 %gather_fusion.2 = f32[8192,2]{1,0:T(8,128)} fusion(f32[2,256]{0,1:T(8,128)S(1)} %bitcast.135, s32[8192]{0:T(1024)S(1)} %broadcast_clamp_fusion), kind=kCustom, calls=%fused_computation.2 | custom fusion | bytes 163840 | tf_op jit(solution)/shard_map/gather | solution.py:77
  699.9 2.9 copy.29
  (767 shorter events, 228.9 us)
Async XLA Ops:
  0.0 334.9 %copy-start = (f32[3,256]{1,0:T(4,128)S(1)}, f32[3,256]{1,0:T(4,128)}, u32[]{:S(2)}) copy-start(f32[3,256]{1,0:T(4,128)} %param.10) | copy-start | bytes 9220
  0.0 183.2 %copy-start.2 = (f32[1,2,256]{2,1,0:T(2,128)S(1)}, f32[1,2,256]{2,1,0:T(2,128)}, u32[]{:S(2)}) copy-start(f32[1,2,256]{2,1,0:T(2,128)} %param.13) | copy-start | bytes 6148
  4.9 644.1 %all-to-all-start = ((s32[128,1,8]{2,1,0:T(1,128)}), s32[128,1,8]{2,1,0:T(1,128)S(1)}, u32[]{:S(2)}, u32[]{:S(2)}) async-start(s32[128,1,8]{2,1,0:T(1,128)} %bitcast.14), calls=%async_computation | async-start | bytes 131072 | tf_op jit(solution)/shard_map/all_to_all | solution.py:120
  653.4 17.2 %all-to-all-start.1 = ((f32[1,2,128,8]{3,1,0,2:T(2,128)}), f32[1,2,128,8]{3,1,0,2:T(2,128)S(1)}, u32[]{:S(2)}, u32[]{:S(2)}) async-start(f32[1,2,128,8]{3,1,0,2:T(2,128)} %bitcast.18), calls=%async_computation.1 | async-start | bytes 262144 | tf_op jit(solution)/shard_map/all_to_all | solution.py:122
  699.9 2.9 copy-start.1
where the time goes:
time: 704 us; the launch traced here: 703 us
  blocking collectives  312 us (44%)
  other arithmetic  179 us (25%)
  matrix products  133 us (19%)
  local copies, waits for them, and re-layouts  42.6 us (6%)
  starting transfers between devices  20.2 us (3%)
  waiting for transfers between devices  11.9 us (2%)
    all_gather x1, blocking collectives, on_device(): lax.all_gather(geometry, 'blk', axis=1, tiled=True)  160 us
    mul x64, other arithmetic, kernel_tile(): weight * (double * (sines - phases * cosine) - COUPLE * single * cosine)  152 us
    all_gather x1, blocking collectives, on_device(): lax.all_gather(send_density, 'blk', axis=1, tiled=True)  152 us
    dot_general x64, matrix products, apply_tile(): jnp.einsum('ts,rs->rt', imag_part, src_imag, precision=highest)  33.7 us
    dot_general x64, matrix products, apply_tile(): jnp.einsum('ts,rs->rt', imag_part, src_real, precision=highest)  33.6 us
    dot_general x64, matrix products, apply_tile(): jnp.einsum('ts,rs->rt', real_part, src_real, precision=highest)  33.6 us
    dot_general x64, matrix products, apply_tile(): jnp.einsum('ts,rs->rt', real_part, src_imag, precision=highest)  32.5 us
    gather x2, local copies, waits for them, and re-layouts, near_field(): looked = needed[:, :, near_rows]  30.6 us
  transfers between devices with their start and end apart: 2, of which 1 were waited for; matrix products, arithmetic and copies ran while one was open for 45% of the time, Pallas kernels for 0%

commit v1 on v0

--- a/solution.py
+++ b/solution.py
@@ -8,6 +8,13 @@
 COUPLE = 1.0
 SOFT = 0.1
 TILE = 512
+
+
+def exchange_gather(array, axis, along):
+    count = lax.axis_size(axis)
+    pieces = jnp.stack([array for _ in range(count)])
+    pieces = lax.all_to_all(pieces, axis, split_axis=0, concat_axis=0)
+    return jnp.concatenate(pieces, axis=along)
 
 
 def unit_normals(angles):
@@ -100,7 +107,7 @@
     far_real, far_imag = far_piece(
         (empty_sum, empty_sum),
         positions,
-        lax.all_gather(geometry, "blk", axis=1, tiled=True),
+        exchange_gather(geometry, "blk", 1),
         lax.all_gather(send_density, "blk", axis=1, tiled=True),
     )
     near_sides = densities.shape[0]

time: 704 us -> 578 us (0.82)
  blocking collectives: 312 us -> 171 us
  waiting for transfers between devices: 11.9 us -> 20.7 us
    all_gather x1 -> x0, blocking collectives: 160 us -> none  [on_device(): lax.all_gather(geometry, 'blk', axis=1, tiled=True)]
    all_gather x1, blocking collectives: 152 us -> 171 us  [on_device(): lax.all_gather(send_density, 'blk', axis=1, tiled=True)]
    all_to_all x1, waiting for transfers between devices: 0.01 us -> 8.91 us  [on_device(): lax.all_to_all(requests, 'blk', split_axis=0, concat_axis=0, tiled=True)]
  transfers between devices with their start and end apart: 2 -> 3, of which waited for: 1 -> 2; matrix products, arithmetic and copies ran while one was open for 45% -> 6% of each run, Pallas kernels for 0% -> 0%
where the time goes in v1:
time: 578 us; the launch traced here: 577 us
  other arithmetic  178 us (31%)
  blocking collectives  171 us (30%)
  matrix products  133 us (23%)
  local copies, waits for them, and re-layouts  43.6 us (8%)
  starting transfers between devices  26.2 us (5%)
  waiting for transfers between devices  20.7 us (4%)
    all_gather x1, blocking collectives, on_device(): lax.all_gather(send_density, 'blk', axis=1, tiled=True)  171 us
    mul x64, other arithmetic, kernel_tile(): weight * (double * (sines - phases * cosine) - COUPLE * single * cosine)  152 us
    dot_general x64, matrix products, apply_tile(): jnp.einsum('ts,rs->rt', imag_part, src_imag, precision=highest)  33.7 us
    dot_general x64, matrix products, apply_tile(): jnp.einsum('ts,rs->rt', imag_part, src_real, precision=highest)  33.6 us
    dot_general x64, matrix products, apply_tile(): jnp.einsum('ts,rs->rt', real_part, src_real, precision=highest)  33.6 us
    dot_general x64, matrix products, apply_tile(): jnp.einsum('ts,rs->rt', real_part, src_imag, precision=highest)  32.5 us
    gather x2, local copies, waits for them, and re-layouts, near_field(): looked = needed[:, :, near_rows]  30.6 us
    reduce_sum x64, other arithmetic, kernel_tile(): facing = jnp.sum(offset_vec * geometry[3:6, None, :], 0)  19.8 us
  transfers between devices with their start and end apart: 3, of which 2 were waited for; matrix products, arithmetic and copies ran while one was open for 6% of the time, Pallas kernels for 0%

profile of v1, /device:TPU:1, one launch (start us, length us, event | category | flops | bytes accessed | tf_op | source)
XLA Modules:
  0.0 576.7 jit_solution(6609428031072205278)
XLA Ops:
  4.9 14.9 %all-to-all-start.1 = ((s32[128,1,8]{2,1,0:T(1,128)}), s32[128,1,8]{2,1,0:T(1,128)S(1)}, u32[]{:S(2)}, u32[]{:S(2)}) async-start(s32[128,1,8]{2,1,0:T(1,128)} %bitcast.15), calls=%async_computation.1 | async-start | bytes 131072 | tf_op jit(solution)/shard_map/all_to_all | solution.py:127
  21.5 8.9 %all-to-all-done.1 = s32[128,1,8]{2,1,0:T(1,128)S(1)} async-done(((s32[128,1,8]{2,1,0:T(1,128)}), s32[128,1,8]{2,1,0:T(1,128)S(1)}, u32[]{:S(2)}, u32[]{:S(2)}) %all-to-all-start.1) | async-done | bytes 4128 | tf_op jit(solution)/shard_map/all_to_all | solution.py:127
  30.5 2.8 gather_fusion
  34.8 5.8 %all-to-all-start.2 = ((f32[1,2,128,8]{3,1,0,2:T(2,128)}), f32[1,2,128,8]{3,1,0,2:T(2,128)S(1)}, u32[]{:S(2)}, u32[]{:S(2)}) async-start(f32[1,2,128,8]{3,1,0,2:T(2,128)} %bitcast.19), calls=%async_computation.2 | async-start | bytes 262144 | tf_op jit(solution)/shard_map/all_to_all | solution.py:129
  40.6 11.8 %all-to-all-done.2 = f32[1,2,128,8]{3,1,0,2:T(2,128)S(1)} async-done(((f32[1,2,128,8]{3,1,0,2:T(2,128)}), f32[1,2,128,8]{3,1,0,2:T(2,128)S(1)}, u32[]{:S(2)}, u32[]{:S(2)}) %all-to-all-start.2) | async-done | bytes 8224 | tf_op jit(solution)/shard_map/all_to_all | solution.py:129
  53.5 5.6 all-to-all-start
  59.2 170.8 %all-gather = f32[1,2,32768]{2,1,0:T(2,128)S(1)} all-gather(f32[1,2,256]{2,1,0:T(2,128)S(1)} %copy-done.3), channel_id=2, replica_groups=mesh['blk'=128,'rhs'=2] {'blk'}, dimensions={2}, use_global_device_ids=true | all-gather | bytes 264192 | tf_op jit(solution)/shard_map/all_gather | solution.py:111
  231.5 27.7 %gather_fusion.2 = f32[8192,2]{1,0:T(8,128)} fusion(f32[2,256]{0,1:T(8,128)S(1)} %bitcast.137, s32[8192]{0:T(1024)S(1)} %broadcast_clamp_fusion), kind=kCustom, calls=%fused_computation.2 | custom fusion | bytes 163840 | tf_op jit(solution)/shard_map/gather | solution.py:84
  259.2 2.9 copy.29
  262.1 313.9 %while.13 = (s32[]{:T(128)}, f32[1,256]{1,0:T(1,128)S(1)}, f32[1,256]{1,0:T(1,128)S(1)}, f32[64,1,2,512]{3,2,1,0:T(2,128)S(1)}, f32[64,7,512]{2,1,0:T(8,128)S(1)...) while((s32[]{:T(128)}, f32[1,256]{1,0:T(1,128)S(1)}, f32[1,256]{1,0:T(1,128)S(1)}, ...), condition=%wide.region_3.4_spmd.clone, body=%wide.region_0.3_spmd.clone.sunk | while | flops 10487301 | bytes 5321883 | solution.py:79
  262.5 2.4 subtract_multiply_fusion.4
  267.4 2.4 subtract_multiply_fusion.4
  272.3 2.4 subtract_multiply_fusion.4
  277.2 2.4 subtract_multiply_fusion.4
  282.1 2.4 subtract_multiply_fusion.4
  287.0 2.4 subtract_multiply_fusion.4
  296.8 2.4 subtract_multiply_fusion.4
  301.8 2.4 subtract_multiply_fusion.4
  306.7 2.4 subtract_multiply_fusion.4
  311.6 2.4 subtract_multiply_fusion.4
  316.5 2.4 subtract_multiply_fusion.4
  321.4 2.4 subtract_multiply_fusion.4
  326.3 2.4 subtract_multiply_fusion.4
  331.2 2.4 subtract_multiply_fusion.4
  336.1 2.4 subtract_multiply_fusion.4
  341.0 2.4 subtract_multiply_fusion.4
  345.9 2.4 subtract_multiply_fusion.4
  350.8 2.4 subtract_multiply_fusion.4
  355.7 2.4 subtract_multiply_fusion.4
  360.6 2.4 subtract_multiply_fusion.4
  365.5 2.4 subtract_multiply_fusion.4
  370.4 2.4 subtract_multiply_fusion.4
  375.3 2.4 subtract_multiply_fusion.4
  380.2 2.4 subtract_multiply_fusion.4
  390.0 2.4 subtract_multiply_fusion.4
  395.0 2.4 subtract_multiply_fusion.4
  399.9 2.4 subtract_multiply_fusion.4
  404.8 2.4 subtract_multiply_fusion.4
  409.7 2.4 subtract_multiply_fusion.4
  414.6 2.4 subtract_multiply_fusion.4
  419.5 2.4 subtract_multiply_fusion.4
  424.4 2.4 subtract_multiply_fusion.4
  429.3 2.4 subtract_multiply_fusion.4
  434.2 2.4 subtract_multiply_fusion.4
  439.1 2.4 subtract_multiply_fusion.4
  444.0 2.4 subtract_multiply_fusion.4
  448.9 2.4 subtract_multiply_fusion.4
  453.8 2.4 subtract_multiply_fusion.4
  (773 shorter events, 230.9 us)
Async XLA Ops:
  1.1 39.5 %copy-start.4 = (f32[256]{0:T(256)S(1)}, f32[256]{0:T(256)}, u32[]{:S(2)}) copy-start(f32[256]{0:T(256)} %param.12) | copy-start | bytes 3076
  1.1 39.5 %copy-start = (f32[3,256]{1,0:T(4,128)S(1)}, f32[3,256]{1,0:T(4,128)}, u32[]{:S(2)}) copy-start(f32[3,256]{1,0:T(4,128)} %param.10) | copy-start | bytes 9220
  4.9 25.4 %all-to-all-start.1 = ((s32[128,1,8]{2,1,0:T(1,128)}), s32[128,1,8]{2,1,0:T(1,128)S(1)}, u32[]{:S(2)}, u32[]{:S(2)}) async-start(s32[128,1,8]{2,1,0:T(1,128)} %bitcast.15), calls=%async_computation.1 | async-start | bytes 131072 | tf_op jit(solution)/shard_map/all_to_all | solution.py:127
  34.8 17.7 %all-to-all-start.2 = ((f32[1,2,128,8]{3,1,0,2:T(2,128)}), f32[1,2,128,8]{3,1,0,2:T(2,128)S(1)}, u32[]{:S(2)}, u32[]{:S(2)}) async-start(f32[1,2,128,8]{3,1,0,2:T(2,128)} %bitcast.19), calls=%async_computation.2 | async-start | bytes 262144 | tf_op jit(solution)/shard_map/all_to_all | solution.py:129
  40.6 18.5 %copy-start.2 = (s32[32,256]{1,0:T(8,128)S(1)}, s32[32,256]{1,0:T(8,128)}, u32[]{:S(2)}) copy-start(s32[32,256]{1,0:T(8,128)} %param.16) | copy-start | bytes 98308
  40.6 18.5 %copy-start.3 = (f32[1,2,256]{2,1,0:T(2,128)S(1)}, f32[1,2,256]{2,1,0:T(2,128)}, u32[]{:S(2)}) copy-start(f32[1,2,256]{2,1,0:T(2,128)} %param.13) | copy-start | bytes 6148
  53.5 208.7 %all-to-all-start = ((f32[128,7,256]{2,1,0:T(8,128)}), f32[128,7,256]{2,1,0:T(8,128)S(1)}, u32[]{:S(2)}, u32[]{:S(2)}) async-start(f32[128,7,256]{2,1,0:T(8,128)} %stack.8), calls=%async_computation | async-start | bytes 2097152 | tf_op jit(solution)/shard_map/all_to_all | solution.py:16
  259.2 2.9 copy-start.1
